TPU v7x, 32 devices: a whole 2x2x4 slice. The times are simulated.
32 devices in a mesh: groups: 2 (over y), seq: 4 (over z), head: 4 (over x, core).
Axes of the slice: x: 2, y: 2, z: 4, core: 2. Of those that a mesh axis runs over, the one named last changes fastest.
Arguments:
- queries: bfloat16 [4096, 2048], P(('groups', 'seq'), 'head'), parts along dimension 0, may hold values from -8 to 8
- keys: bfloat16 [4096, 2048], P(('groups', 'seq'), 'head'), parts along dimension 0, may hold values from -8 to 8
- values: bfloat16 [4096, 2048], P(('groups', 'seq'), 'head'), parts along dimension 0, may hold values from -12 to 12
- w_out: bfloat16 [2048, 2048], replicated, may hold values from -0.125 to 0.125
Outputs:
- projected: bfloat16 [4096, 2048], P(('groups', 'seq', 'head')), parts along dimension 0
There are 2 independent parts, one for each index of `groups`. A program takes and returns all parts, laid end to end along the dimension named above; an argument that names none is the same for every part. Nothing has to cross between parts.
All inputs are finite; a program needn't handle non-finite values.
Results may differ from a plain program's by a relative error of at most 0.005.
Values may be sent and summed in bfloat16 or wider, within the bound.
A program may use at most 128 MiB of HBM per device.

v0:
```python
import math
import jax
import jax.numpy as jnp
from jax import lax
from jax.sharding import PartitionSpec as P

HD = 128
WINDOW = 2048


def shifted(value, axis, steps):
    count = lax.axis_size(axis)
    first, last = (max(0, -steps), min(count, count - steps))
    return lax.ppermute(value, axis, [(source, source + steps) for source in range(first, last)])


def per_device(queries, keys, values, w_out):
    length_dev, width = queries.shape
    heads_dev = width // HD
    block_rows = min(512, length_dev)
    block_count = length_dev // block_rows
    highest = lax.Precision.HIGHEST
    seq_index = lax.axis_index("seq")
    q_blocks = queries.reshape(block_count, block_rows, heads_dev, HD)
    k_blocks = keys.reshape(block_count, block_rows, heads_dev, HD)
    v_blocks = values.reshape(block_count, block_rows, heads_dev, HD)
    block_states = jnp.einsum(
        "bkhd,bkhe->bhde", k_blocks, v_blocks, preferred_element_type=jnp.float32
    )
    own_state = jnp.sum(block_states, axis=0)
    earlier = jnp.cumsum(block_states, axis=0) - block_states
    piece = lax.all_gather(own_state[None], "seq", axis=0, tiled=True)
    order = jnp.arange(piece.shape[0], dtype=jnp.int32)
    keep = order < seq_index
    prefix = jnp.sum(jnp.where(keep[:, None, None, None], piece, 0.0), axis=0)
    causal = jnp.arange(block_rows)[:, None] >= jnp.arange(block_rows)[None, :]
    local_scores = jnp.einsum(
        "bqhd,bkhd->bhqk", q_blocks, k_blocks, preferred_element_type=jnp.float32
    )
    local_scores = jnp.where(causal, local_scores, 0.0)
    intra = jnp.einsum(
        "bhqk,bkhe->bqhe", local_scores, v_blocks.astype(jnp.float32), precision=highest
    )
    state_before = prefix[None] + earlier
    inter = jnp.einsum(
        "bqhd,bhde->bqhe", q_blocks.astype(jnp.float32), state_before, precision=highest
    )
    linear = (intra + inter).reshape(length_dev, heads_dev, HD)
    normed = linear / jnp.sqrt(jnp.mean(linear * linear, axis=-1, keepdims=True) + 1e-06)
    reach = min(WINDOW // length_dev, lax.axis_size("seq") - 1)
    received = [shifted((keys, values), "seq", distance) for distance in range(1, reach + 1)]
    pad_rows = WINDOW - reach * length_dev
    filler = jnp.zeros((pad_rows, width), keys.dtype)
    wide_keys = jnp.concatenate([filler] + [pair[0] for pair in reversed(received)] + [keys], 0)
    wide_values = jnp.concatenate([filler] + [pair[1] for pair in reversed(received)] + [values], 0)
    wide_keys = wide_keys.reshape(-1, heads_dev, HD)
    wide_values = wide_values.reshape(-1, heads_dev, HD)
    scale = 1.0 / math.sqrt(HD)
    span = WINDOW + block_rows
    query_pos = jnp.arange(block_rows, dtype=jnp.int32)[:, None]
    key_pos = jnp.arange(span, dtype=jnp.int32)[None, :]
    band = (key_pos > query_pos) & (key_pos <= query_pos + WINDOW)
    rows_q = queries.reshape(block_rows, heads_dev, HD)
    anchor = seq_index * length_dev + 0 - WINDOW
    valid = band & (anchor + key_pos >= 0)
    scores = (
        jnp.einsum("qhd,khd->hqk", rows_q, wide_keys, preferred_element_type=jnp.float32) * scale
    )
    scores = jnp.where(valid[None], scores, -1e30)
    top = jnp.max(scores, axis=-1, keepdims=True)
    expo = jnp.where(valid[None], jnp.exp(scores - top), 0.0)
    total = jnp.sum(expo, axis=-1)
    weights = expo.astype(jnp.bfloat16)
    summed = jnp.einsum("hqk,khe->qhe", weights, wide_values, preferred_element_type=jnp.float32)
    pieces = summed / jnp.transpose(total)[:, :, None]
    mixed = (normed + pieces).astype(jnp.bfloat16).reshape(length_dev, width)
    head_count = lax.axis_size("head")
    share = length_dev // head_count
    grouped = mixed.reshape(head_count, share, width)
    return jnp.dot(
        lax.all_to_all(grouped, "head", split_axis=0, concat_axis=2, tiled=True)[0],
        w_out,
        preferred_element_type=jnp.float32,
    ).astype(jnp.bfloat16)


def solution(mesh):
    return jax.shard_map(
        per_device,
        mesh=mesh,
        in_specs=(
            P(("groups", "seq"), "head"),
            P(("groups", "seq"), "head"),
            P(("groups", "seq"), "head"),
            P(),
        ),
        out_specs=P(("groups", "seq", "head"), None),
        check_vma=False,
    )
```

profile of v0, /device:TPU:16, one launch (start us, length us, event | category | flops | bytes accessed | tf_op | source)
XLA Modules:
  0.0 174.5 jit_solution(8869428141898482623)
XLA Ops:
  6.5 1.3 copy.52
  7.9 1.5 collective-permute-start.3
  9.3 1.3 collective-permute-start.4
  10.6 3.3 %collective-permute-start.5 = (bf16[512,512]{0,1:T(8,128)(2,1)S(1)}, bf16[512,512]{0,1:T(8,128)(2,1)}, u32[]{:S(2)}, u32[]{:S(2)}) collective-permute-start(bf16[512,512]{0,1:T(8,128)(2,1)S(1)} %copy.52), channel_id=1, source_target_pairs={{0,4},{4,8},{8,12},{1,5},{5,9},{9,13},{2,6},{6,10},{10,14},{3,7},{... | collective-permute-start | bytes 1572872 | tf_op jit(solution)/shard_map/ppermute | solution.py:14
  13.9 1.3 copy.37
  15.2 1.5 collective-permute-start
  16.7 1.3 collective-permute-start.1
  18.0 2.0 %fusion.37 = f32[4,128,128]{2,1,0:T(8,128)} fusion(bf16[512,4,128]{0,2,1:T(8,128)(2,1)S(1)} %bitcast.96, bf16[512,512]{1,0:T(8,128)(2,1)} %param.6), kind=kOutput, calls=%fused_computation.30 | convolution fusion | flops 67108864 | bytes 1310720 | tf_op jit(solution)/shard_map/bkhd,bkhe->bhde/dot_general | solution.py:27
  20.0 0.0 all-gather.3.cloned.1.call-update
  20.1 1.9 %fusion.8 = pred[512,2560]{0,1:T(8,128)(4,1)S(1)} fusion(s32[512]{0:T(512)S(1)} %iota_add_fusion, pred[2560]{0:T(1024)(128)(4,1)S(1)} %add_compare_fusion), kind=kLoop, calls=%fused_computation.12 | loop fusion | flops 5242880 | bytes 1315328 | tf_op jit(solution)/shard_map/and | solution.py:65
  22.0 2.8 %fusion.46 = f32[4,512,512]{2,1,0:T(8,128)} fusion(bf16[512,4,128]{0,2,1:T(8,128)(2,1)S(1)} %bitcast.97, bf16[512,512]{1,0:T(8,128)(2,1)S(1)} %copy-done), kind=kOutput, calls=%fused_computation.37 | convolution fusion | flops 268435456 | bytes 5242880 | tf_op jit(solution)/shard_map/bqhd,bkhd->bhqk/dot_general | solution.py:37
  24.8 0.1 iota_compare_fusion.2
  24.9 0.0 collective-permute-done.3
  24.9 5.3 %collective-permute-start.2 = (bf16[512,512]{0,1:T(8,128)(2,1)S(1)}, bf16[512,512]{0,1:T(8,128)(2,1)S(1)}, u32[]{:S(2)}, u32[]{:S(2)}) collective-permute-start(bf16[512,512]{0,1:T(8,128)(2,1)S(1)} %copy.37), channel_id=1, source_target_pairs={{0,4},{4,8},{8,12},{1,5},{5,9},{9,13},{2,6},{6,10},{10,14},{3,7},{... | collective-permute-start | bytes 1572872 | tf_op jit(solution)/shard_map/ppermute | solution.py:14
  30.2 1.1 constant_dynamic-update-slice_fusion.7
  31.3 10.9 %collective-permute-done.4 = bf16[512,512]{0,1:T(8,128)(2,1)} collective-permute-done((bf16[512,512]{0,1:T(8,128)(2,1)S(1)}, bf16[512,512]{0,1:T(8,128)(2,1)}, u32[]{:S(2)}, u32[]{:S(2)}) %collective-permute-start.4) | collective-permute-done | bytes 524320 | tf_op jit(solution)/shard_map/ppermute | solution.py:14
  42.2 1.1 constant_dynamic-update-slice_fusion.6
  43.3 55.3 %collective-permute-done.5 = bf16[512,512]{0,1:T(8,128)(2,1)} collective-permute-done((bf16[512,512]{0,1:T(8,128)(2,1)S(1)}, bf16[512,512]{0,1:T(8,128)(2,1)}, u32[]{:S(2)}, u32[]{:S(2)}) %collective-permute-start.5) | collective-permute-done | bytes 524320 | tf_op jit(solution)/shard_map/ppermute | solution.py:14
  98.6 1.1 constant_dynamic-update-slice_fusion.5
  99.7 1.5 constant_dynamic-update-slice_fusion.3
  101.2 1.1 constant_dynamic-update-slice_fusion.2
  102.3 18.6 %collective-permute-done.2 = bf16[512,512]{0,1:T(8,128)(2,1)S(1)} collective-permute-done((bf16[512,512]{0,1:T(8,128)(2,1)S(1)}, bf16[512,512]{0,1:T(8,128)(2,1)S(1)}, u32[]{:S(2)}, u32[]{:S(2)}) %collective-permute-start.2) | collective-permute-done | bytes 524320 | tf_op jit(solution)/shard_map/ppermute | solution.py:14
  121.0 1.4 copy-done.3
  122.4 15.3 %fusion.63 = (f32[4,512]{1,0:T(4,128)S(1)}, bf16[4,512,2560]{1,2,0:T(8,128)(2,1)}) fusion(pred[512,2560]{0,1:T(8,128)(4,1)S(1)} %fusion.8, bf16[2560,4,128]{0,2,1:T(8,128)(2,1)} %bitcast.101, bf16[512,512]{1,0:T(8,128)(2,1)S(1)} %copy-done), kind=kOutput, calls=%fused_computation.64 | convolution fusion | flops 1373637120 | bytes 14950400 | tf_op jit(solution)/shard_map/sub | solution.py:71
  137.7 1.4 select_reduce_fusion
  139.2 0.6 fusion.44
  139.8 5.2 %multiply_reduce_fusion = (f32[512,4]{0,1:T(4,128)S(1)}, f32[512,4,128]{0,2,1:T(8,128)S(1)}) fusion(f32[4,128,512]{2,1,0:T(8,128)S(1)} %fusion.44, f32[4,512,512]{2,1,0:T(8,128)} %fusion.46, pred[512,512]{1,0:T(8,128)(4,1)S(1)} %iota_compare_fusion.2, bf16[512,512]{1,0:T(8,128)(2,1)S(1)} %copy-done.1), kind=kOutput, calls=%fused_computation.26 | convolution fusion | flops 1612445696 | bytes 7086080 | tf_op jit(solution)/shard_map/bhqk,bkhe->bqhe/dot_general | solution.py:41
  145.0 5.6 %fusion.33 = bf16[512,4,128]{0,2,1:T(8,128)(2,1)S(1)} fusion(bf16[2560,4,128]{0,2,1:T(8,128)(2,1)S(1)} %bitcast.100, bf16[4,512,2560]{1,2,0:T(8,128)(2,1)} %get-tuple-element.6, f32[512,4,128]{0,2,1:T(8,128)S(1)} %get-tuple-element.8, f32[512,4]{0,1:T(4,128)S(1)} %bitcast.102, f32[512,4]{0,1:T(4,128)S(1)} %add_sqrt_fusion), kind=kOutput, calls=%fused_computation.25 | convolution fusion | flops 1343225856 | bytes 14696448 | tf_op jit(solution)/shard_map/hqk,khe->qhe/dot_general | solution.py:74
  150.6 0.1 reshape_reshape.3
  150.7 0.1 copy.48
  150.8 11.4 %all_to_all.15 = bf16[4,128,512]{1,2,0:T(8,128)(2,1)S(1)} all-to-all(bf16[4,128,512]{1,2,0:T(8,128)(2,1)S(1)} %copy.48), channel_id=1, replica_groups=mesh['groups'=2,'seq'=4,'head'=4] {'head'}, dimensions={0} | all-to-all | bytes 1048576 | tf_op jit(solution)/shard_map/all_to_all | solution.py:81
  162.2 5.5 %convolution_convert_fusion = bf16[128,2048]{1,0:T(8,128)(2,1)} fusion(bf16[128,2048]{0,1:T(8,128)(2,1)S(1)} %bitcast.98, bf16[2048,2048]{1,0:T(8,128)(2,1)} %param.7), kind=kOutput, calls=%fused_computation.15 | convolution fusion | flops 1074003968 | bytes 9437184 | tf_op jit(solution)/shard_map/dot_general | solution.py:80
  (24 shorter events, 0.2 us)
Async XLA Ops:
  6.5 15.4 %copy-start = (bf16[512,512]{1,0:T(8,128)(2,1)S(1)}, bf16[512,512]{1,0:T(8,128)(2,1)}, u32[]{:S(2)}) copy-start(bf16[512,512]{1,0:T(8,128)(2,1)} %param.4) | copy-start | bytes 1572868
  6.5 131.2 %all-gather.3.cloned.1.call-start = ((), (), s32[]{:S(2)}) async-start(), calls=%async_computation.1 | async-start | bytes 1310720 | tf_op jit(solution)/shard_map/all_gather | solution.py:32
  7.9 17.1 %collective-permute-start.3 = (bf16[512,512]{0,1:T(8,128)(2,1)S(1)}, bf16[512,512]{0,1:T(8,128)(2,1)}, u32[]{:S(2)}, u32[]{:S(2)}) collective-permute-start(bf16[512,512]{0,1:T(8,128)(2,1)S(1)} %copy.52), channel_id=1, source_target_pairs={{0,12},{1,13},{2,14},{3,15},{16,28},{17,29},{18,30},{19,31}} | collective-permute-start | bytes 1572872 | tf_op jit(solution)/shard_map/ppermute | solution.py:14
  9.3 32.9 %collective-permute-start.4 = (bf16[512,512]{0,1:T(8,128)(2,1)S(1)}, bf16[512,512]{0,1:T(8,128)(2,1)}, u32[]{:S(2)}, u32[]{:S(2)}) collective-permute-start(bf16[512,512]{0,1:T(8,128)(2,1)S(1)} %copy.52), channel_id=1, source_target_pairs={{0,8},{4,12},{1,9},{5,13},{2,10},{6,14},{3,11},{7,15},{16,24},{20,... | collective-permute-start | bytes 1572872 | tf_op jit(solution)/shard_map/ppermute | solution.py:14
  10.6 88.0 %collective-permute-start.5 = (bf16[512,512]{0,1:T(8,128)(2,1)S(1)}, bf16[512,512]{0,1:T(8,128)(2,1)}, u32[]{:S(2)}, u32[]{:S(2)}) collective-permute-start(bf16[512,512]{0,1:T(8,128)(2,1)S(1)} %copy.52), channel_id=1, source_target_pairs={{0,4},{4,8},{8,12},{1,5},{5,9},{9,13},{2,6},{6,10},{10,14},{3,7},{... | collective-permute-start | bytes 1572872 | tf_op jit(solution)/shard_map/ppermute | solution.py:14
  15.2 84.5 %collective-permute-start = (bf16[512,512]{0,1:T(8,128)(2,1)S(1)}, bf16[512,512]{0,1:T(8,128)(2,1)}, u32[]{:S(2)}, u32[]{:S(2)}) collective-permute-start(bf16[512,512]{0,1:T(8,128)(2,1)S(1)} %copy.37), channel_id=1, source_target_pairs={{0,12},{1,13},{2,14},{3,15},{16,28},{17,29},{18,30},{19,31}} | collective-permute-start | bytes 1572872 | tf_op jit(solution)/shard_map/ppermute | solution.py:14
  16.7 84.5 %collective-permute-start.1 = (bf16[512,512]{0,1:T(8,128)(2,1)S(1)}, bf16[512,512]{0,1:T(8,128)(2,1)}, u32[]{:S(2)}, u32[]{:S(2)}) collective-permute-start(bf16[512,512]{0,1:T(8,128)(2,1)S(1)} %copy.37), channel_id=1, source_target_pairs={{0,8},{4,12},{1,9},{5,13},{2,10},{6,14},{3,11},{7,15},{16,24},{20,... | collective-permute-start | bytes 1572872 | tf_op jit(solution)/shard_map/ppermute | solution.py:14
  24.9 95.9 %collective-permute-start.2 = (bf16[512,512]{0,1:T(8,128)(2,1)S(1)}, bf16[512,512]{0,1:T(8,128)(2,1)S(1)}, u32[]{:S(2)}, u32[]{:S(2)}) collective-permute-start(bf16[512,512]{0,1:T(8,128)(2,1)S(1)} %copy.37), channel_id=1, source_target_pairs={{0,4},{4,8},{8,12},{1,5},{5,9},{9,13},{2,6},{6,10},{10,14},{3,7},{... | collective-permute-start | bytes 1572872 | tf_op jit(solution)/shard_map/ppermute | solution.py:14
  99.7 21.2 %copy-start.5 = (bf16[2560,512]{0,1:T(8,128)(2,1)}, bf16[2560,512]{0,1:T(8,128)(2,1)S(1)}, u32[]{:S(2)}) copy-start(bf16[2560,512]{0,1:T(8,128)(2,1)S(1)} %constant_dynamic-update-slice_fusion.4) | copy-start | bytes 7864324
  121.0 1.5 copy-start.3
  122.4 16.8 %copy-start.2 = (f32[4,128,128]{2,1,0:T(8,128)S(1)}, f32[4,128,128]{2,1,0:T(8,128)}, u32[]{:S(2)}) copy-start(f32[4,128,128]{2,1,0:T(8,128)} %fusion.37) | copy-start | bytes 786436
  137.7 2.1 %copy-start.1 = (bf16[512,512]{1,0:T(8,128)(2,1)S(1)}, bf16[512,512]{1,0:T(8,128)(2,1)}, u32[]{:S(2)}) copy-start(bf16[512,512]{1,0:T(8,128)(2,1)} %param.6) | copy-start | bytes 1572868
  139.8 5.2 %copy-start.4 = (bf16[2560,512]{0,1:T(8,128)(2,1)S(1)}, bf16[2560,512]{0,1:T(8,128)(2,1)}, u32[]{:S(2)}) copy-start(bf16[2560,512]{0,1:T(8,128)(2,1)} %copy-done.3) | copy-start | bytes 7864324
Sparse Core Ops, SparseCore 0:
  20.2 60.3 all-gather.2
where the time goes:
time: 175 us; the launch traced here: 174 us
  waiting for transfers between devices  84.8 us (48%)
  matrix products  36.9 us (21%)
  starting transfers between devices  14.2 us (8%)
  between operations  13.7 us (8%)
  blocking collectives  11.4 us (7%)
  local copies, waits for them, and re-layouts  10.2 us (6%)
  other arithmetic  3.42 us (2%)
    ppermute x6, waiting for transfers between devices, shifted(): lax.ppermute(value, axis, [(source, source + steps) for source in range(f...  84.7 us
    sub x1, matrix products, per_device(): expo = jnp.where(valid[None], jnp.exp(scores - top), 0.0)  15.3 us
    ppermute x6, starting transfers between devices, shifted(): lax.ppermute(value, axis, [(source, source + steps) for source in range(f...  14.2 us
    all_to_all x1, blocking collectives, per_device(): lax.all_to_all(grouped, 'head', split_axis=0, concat_axis=2, tiled=True)[0]  11.4 us
    unnamed x21, local copies, waits for them, and re-layouts  8.63 us
    dot_general x1, matrix products, per_device(): jnp.einsum('hqk,khe->qhe', weights, wide_values, preferred_element_type=j...  5.56 us
    dot_general x1, matrix products, per_device(): jnp.dot(lax.all_to_all(grouped, 'head', split_axis=0, concat_axis=2, tile...  5.46 us
    dot_general x1, matrix products, per_device(): jnp.einsum('bhqk,bkhe->bqhe', local_scores, v_blocks.astype(jnp.float32),...  5.17 us
  transfers between devices with their start and end apart: 7, of which 3 were waited for; matrix products, arithmetic and copies ran while one was open for 17% of the time, Pallas kernels for 0%

commit v1 on v0

--- a/solution.py
+++ b/solution.py
@@ -3,6 +3,7 @@
 import jax.numpy as jnp
 from jax import lax
 from jax.sharding import PartitionSpec as P
+from jax.lax import all_to_all, axis_size
 
 HD = 128
 WINDOW = 2048
@@ -15,6 +16,15 @@
 
 
 def per_device(queries, keys, values, w_out):
+
+    def rest_bars_on_mesh(w_in, ax_name):
+        return jnp.concatenate(
+            all_to_all(
+                jnp.stack(jnp.split(w_in, axis_size(ax_name), axis=0), axis=0), ax_name, 0, 0
+            ),
+            axis=2,
+        )
+
     length_dev, width = queries.shape
     heads_dev = width // HD
     block_rows = min(512, length_dev)
@@ -78,9 +88,7 @@
     share = length_dev // head_count
     grouped = mixed.reshape(head_count, share, width)
     return jnp.dot(
-        lax.all_to_all(grouped, "head", split_axis=0, concat_axis=2, tiled=True)[0],
-        w_out,
-        preferred_element_type=jnp.float32,
+        rest_bars_on_mesh(grouped, "head")[0], w_out, preferred_element_type=jnp.float32
     ).astype(jnp.bfloat16)
 
 

time: 175 us -> 172 us (0.983)
  matrix products: 36.9 us -> 33.7 us
    dot_general x1, matrix products: 5.46 us -> 2.09 us  [per_device(): jnp.dot(rest_bars_on_mesh(grouped, 'head')[0], w_out, preferred_element_t...]
    unnamed x21 -> x25, local copies, waits for them, and re-layouts: 8.63 us -> 8.65 us
where the time goes in v1:
time: 172 us; the launch traced here: 171 us
  waiting for transfers between devices  84.7 us (49%)
  matrix products  33.7 us (20%)
  starting transfers between devices  14.2 us (8%)
  between operations  13.7 us (8%)
  blocking collectives  11.4 us (7%)
  local copies, waits for them, and re-layouts  10.1 us (6%)
  other arithmetic  3.49 us (2%)
    ppermute x6, waiting for transfers between devices, shifted(): lax.ppermute(value, axis, [(source, source + steps) for source in range(f...  84.7 us
    sub x1, matrix products, per_device(): expo = jnp.where(valid[None], jnp.exp(scores - top), 0.0)  15.3 us
    ppermute x6, starting transfers between devices, shifted(): lax.ppermute(value, axis, [(source, source + steps) for source in range(f...  14.2 us
    all_to_all x1, blocking collectives, rest_bars_on_mesh(): all_to_all(jnp.stack(jnp.split(w_in, axis_size(ax_name), axis=0), axis=0)...  11.4 us
    unnamed x25, local copies, waits for them, and re-layouts  8.65 us
    dot_general x1, matrix products, per_device(): jnp.einsum('hqk,khe->qhe', weights, wide_values, preferred_element_type=j...  5.71 us
    dot_general x1, matrix products, per_device(): jnp.einsum('bhqk,bkhe->bqhe', local_scores, v_blocks.astype(jnp.float32),...  5.17 us
  transfers between devices with their start and end apart: 7, of which 3 were waited for; matrix products, arithmetic and copies ran while one was open for 17% of the time, Pallas kernels for 0%

profile of v1, /device:TPU:16, one launch (start us, length us, event | category | flops | bytes accessed | tf_op | source)
XLA Modules:
  0.0 171.3 jit_solution(7335458259961436119)
XLA Ops:
  6.5 1.3 copy.50
  7.9 1.5 collective-permute-start.3
  9.3 1.3 collective-permute-start.4
  10.6 3.3 %collective-permute-start.5 = (bf16[512,512]{0,1:T(8,128)(2,1)S(1)}, bf16[512,512]{0,1:T(8,128)(2,1)}, u32[]{:S(2)}, u32[]{:S(2)}) collective-permute-start(bf16[512,512]{0,1:T(8,128)(2,1)S(1)} %copy.50), channel_id=1, source_target_pairs={{0,4},{4,8},{8,12},{1,5},{5,9},{9,13},{2,6},{6,10},{10,14},{3,7},{... | collective-permute-start | bytes 1572872 | tf_op jit(solution)/shard_map/ppermute | solution.py:15
  13.9 1.3 copy.36
  15.2 1.5 collective-permute-start
  16.7 1.3 collective-permute-start.1
  18.0 2.0 %fusion.37 = f32[4,128,128]{2,1,0:T(8,128)} fusion(bf16[512,4,128]{0,2,1:T(8,128)(2,1)S(1)} %bitcast.98, bf16[512,512]{1,0:T(8,128)(2,1)} %param.6), kind=kOutput, calls=%fused_computation.30 | convolution fusion | flops 67108864 | bytes 1310720 | tf_op jit(solution)/shard_map/bkhd,bkhe->bhde/dot_general | solution.py:37
  20.0 0.0 all-gather.3.cloned.1.call-update
  20.1 1.9 %fusion.8 = pred[512,2560]{0,1:T(8,128)(4,1)S(1)} fusion(s32[512]{0:T(512)S(1)} %iota_add_fusion, pred[2560]{0:T(1024)(128)(4,1)S(1)} %add_compare_fusion), kind=kLoop, calls=%fused_computation.12 | loop fusion | flops 5242880 | bytes 1315328 | tf_op jit(solution)/shard_map/and | solution.py:75
  21.9 2.8 %fusion.46 = f32[4,512,512]{2,1,0:T(8,128)} fusion(bf16[512,4,128]{0,2,1:T(8,128)(2,1)S(1)} %bitcast.99, bf16[512,512]{1,0:T(8,128)(2,1)S(1)} %copy-done), kind=kOutput, calls=%fused_computation.37 | convolution fusion | flops 268435456 | bytes 5242880 | tf_op jit(solution)/shard_map/bqhd,bkhd->bhqk/dot_general | solution.py:47
  24.7 0.1 iota_compare_fusion.2
  24.9 5.3 %collective-permute-start.2 = (bf16[512,512]{0,1:T(8,128)(2,1)S(1)}, bf16[512,512]{0,1:T(8,128)(2,1)S(1)}, u32[]{:S(2)}, u32[]{:S(2)}) collective-permute-start(bf16[512,512]{0,1:T(8,128)(2,1)S(1)} %copy.36), channel_id=1, source_target_pairs={{0,4},{4,8},{8,12},{1,5},{5,9},{9,13},{2,6},{6,10},{10,14},{3,7},{... | collective-permute-start | bytes 1572872 | tf_op jit(solution)/shard_map/ppermute | solution.py:15
  30.2 1.1 constant_dynamic-update-slice_fusion.7
  31.3 10.9 %collective-permute-done.4 = bf16[512,512]{0,1:T(8,128)(2,1)} collective-permute-done((bf16[512,512]{0,1:T(8,128)(2,1)S(1)}, bf16[512,512]{0,1:T(8,128)(2,1)}, u32[]{:S(2)}, u32[]{:S(2)}) %collective-permute-start.4) | collective-permute-done | bytes 524320 | tf_op jit(solution)/shard_map/ppermute | solution.py:15
  42.2 1.1 constant_dynamic-update-slice_fusion.6
  43.3 55.3 %collective-permute-done.5 = bf16[512,512]{0,1:T(8,128)(2,1)} collective-permute-done((bf16[512,512]{0,1:T(8,128)(2,1)S(1)}, bf16[512,512]{0,1:T(8,128)(2,1)}, u32[]{:S(2)}, u32[]{:S(2)}) %collective-permute-start.5) | collective-permute-done | bytes 524320 | tf_op jit(solution)/shard_map/ppermute | solution.py:15
  98.6 1.1 constant_dynamic-update-slice_fusion.5
  99.7 1.5 constant_dynamic-update-slice_fusion.3
  101.2 1.1 constant_dynamic-update-slice_fusion.2
  102.3 18.6 %collective-permute-done.2 = bf16[512,512]{0,1:T(8,128)(2,1)S(1)} collective-permute-done((bf16[512,512]{0,1:T(8,128)(2,1)S(1)}, bf16[512,512]{0,1:T(8,128)(2,1)S(1)}, u32[]{:S(2)}, u32[]{:S(2)}) %collective-permute-start.2) | collective-permute-done | bytes 524320 | tf_op jit(solution)/shard_map/ppermute | solution.py:15
  121.0 1.5 copy-done.3
  122.4 15.3 %fusion.64 = (f32[4,512]{1,0:T(4,128)S(1)}, bf16[4,512,2560]{1,2,0:T(8,128)(2,1)}) fusion(pred[512,2560]{0,1:T(8,128)(4,1)S(1)} %fusion.8, bf16[2560,4,128]{0,2,1:T(8,128)(2,1)} %bitcast.107, bf16[512,512]{1,0:T(8,128)(2,1)S(1)} %copy-done), kind=kOutput, calls=%fused_computation.66 | convolution fusion | flops 1373637120 | bytes 14950400 | tf_op jit(solution)/shard_map/sub | solution.py:81
  137.7 1.4 select_reduce_fusion
  139.2 0.6 fusion.44
  139.8 5.2 %multiply_reduce_fusion = (f32[512,4]{0,1:T(4,128)S(1)}, f32[512,4,128]{0,2,1:T(8,128)S(1)}) fusion(f32[4,128,512]{2,1,0:T(8,128)S(1)} %fusion.44, f32[4,512,512]{2,1,0:T(8,128)} %fusion.46, pred[512,512]{1,0:T(8,128)(4,1)S(1)} %iota_compare_fusion.2, bf16[512,512]{1,0:T(8,128)(2,1)S(1)} %copy-done.1), kind=kOutput, calls=%fused_computation.26 | convolution fusion | flops 1612445696 | bytes 7086080 | tf_op jit(solution)/shard_map/bhqk,bkhe->bqhe/dot_general | solution.py:51
  145.0 0.0 slice-start
  145.0 5.7 %fusion.33 = bf16[512,4,128]{0,2,1:T(8,128)(2,1)S(1)} fusion(bf16[2560,4,128]{0,2,1:T(8,128)(2,1)S(1)} %bitcast.106, bf16[4,512,2560]{1,2,0:T(8,128)(2,1)} %get-tuple-element.10, f32[512,4,128]{0,2,1:T(8,128)S(1)} %get-tuple-element.12, f32[512,4]{0,1:T(4,128)S(1)} %bitcast.108, f32[512,4]{0,1:T(4,128)S(1)} %add_sqrt_fusion), kind=kOutput, calls=%fused_computation.25 | convolution fusion | flops 1343225856 | bytes 14696448 | tf_op jit(solution)/shard_map/hqk,khe->qhe/dot_general | solution.py:84
  150.8 0.1 fusion.63
  150.9 0.1 pad_maximum_fusion
  151.0 11.4 %all_to_all.5 = bf16[4,1,128,512]{2,3,1,0:T(8,128)(2,1)S(1)} all-to-all(bf16[4,1,128,512]{2,3,1,0:T(8,128)(2,1)S(1)} %pad_maximum_fusion), channel_id=1, replica_groups=mesh['groups'=2,'seq'=4,'head'=4] {'head'}, dimensions={0} | all-to-all | bytes 1048576 | tf_op jit(solution)/shard_map/all_to_all | solution.py:22
  162.4 2.1 %convolution_convert_fusion = bf16[128,2048]{1,0:T(8,128)(2,1)} fusion(bf16[128,2048]{0,1:T(8,128)(2,1)S(1)} %bitcast.100, bf16[2048,2048]{1,0:T(8,128)(2,1)S(1)} %bitcast.97), kind=kOutput, calls=%fused_computation.15 | convolution fusion | flops 1074003968 | bytes 9437184 | tf_op jit(solution)/shard_map/dot_general | solution.py:90
  (29 shorter events, 0.2 us)
Async XLA Ops:
  6.5 15.4 %copy-start = (bf16[512,512]{1,0:T(8,128)(2,1)S(1)}, bf16[512,512]{1,0:T(8,128)(2,1)}, u32[]{:S(2)}) copy-start(bf16[512,512]{1,0:T(8,128)(2,1)} %param.4) | copy-start | bytes 1572868
  6.5 131.2 %all-gather.3.cloned.1.call-start = ((), (), s32[]{:S(2)}) async-start(), calls=%async_computation.1 | async-start | bytes 1310720 | tf_op jit(solution)/shard_map/all_gather | solution.py:42
  7.9 17.0 %collective-permute-start.3 = (bf16[512,512]{0,1:T(8,128)(2,1)S(1)}, bf16[512,512]{0,1:T(8,128)(2,1)}, u32[]{:S(2)}, u32[]{:S(2)}) collective-permute-start(bf16[512,512]{0,1:T(8,128)(2,1)S(1)} %copy.50), channel_id=1, source_target_pairs={{0,12},{1,13},{2,14},{3,15},{16,28},{17,29},{18,30},{19,31}} | collective-permute-start | bytes 1572872 | tf_op jit(solution)/shard_map/ppermute | solution.py:15
  9.3 32.9 %collective-permute-start.4 = (bf16[512,512]{0,1:T(8,128)(2,1)S(1)}, bf16[512,512]{0,1:T(8,128)(2,1)}, u32[]{:S(2)}, u32[]{:S(2)}) collective-permute-start(bf16[512,512]{0,1:T(8,128)(2,1)S(1)} %copy.50), channel_id=1, source_target_pairs={{0,8},{4,12},{1,9},{5,13},{2,10},{6,14},{3,11},{7,15},{16,24},{20,... | collective-permute-start | bytes 1572872 | tf_op jit(solution)/shard_map/ppermute | solution.py:15
  10.6 88.0 %collective-permute-start.5 = (bf16[512,512]{0,1:T(8,128)(2,1)S(1)}, bf16[512,512]{0,1:T(8,128)(2,1)}, u32[]{:S(2)}, u32[]{:S(2)}) collective-permute-start(bf16[512,512]{0,1:T(8,128)(2,1)S(1)} %copy.50), channel_id=1, source_target_pairs={{0,4},{4,8},{8,12},{1,5},{5,9},{9,13},{2,6},{6,10},{10,14},{3,7},{... | collective-permute-start | bytes 1572872 | tf_op jit(solution)/shard_map/ppermute | solution.py:15
  15.2 84.5 %collective-permute-start = (bf16[512,512]{0,1:T(8,128)(2,1)S(1)}, bf16[512,512]{0,1:T(8,128)(2,1)}, u32[]{:S(2)}, u32[]{:S(2)}) collective-permute-start(bf16[512,512]{0,1:T(8,128)(2,1)S(1)} %copy.36), channel_id=1, source_target_pairs={{0,12},{1,13},{2,14},{3,15},{16,28},{17,29},{18,30},{19,31}} | collective-permute-start | bytes 1572872 | tf_op jit(solution)/shard_map/ppermute | solution.py:15
  16.7 84.5 %collective-permute-start.1 = (bf16[512,512]{0,1:T(8,128)(2,1)S(1)}, bf16[512,512]{0,1:T(8,128)(2,1)}, u32[]{:S(2)}, u32[]{:S(2)}) collective-permute-start(bf16[512,512]{0,1:T(8,128)(2,1)S(1)} %copy.36), channel_id=1, source_target_pairs={{0,8},{4,12},{1,9},{5,13},{2,10},{6,14},{3,11},{7,15},{16,24},{20,... | collective-permute-start | bytes 1572872 | tf_op jit(solution)/shard_map/ppermute | solution.py:15
  24.9 96.0 %collective-permute-start.2 = (bf16[512,512]{0,1:T(8,128)(2,1)S(1)}, bf16[512,512]{0,1:T(8,128)(2,1)S(1)}, u32[]{:S(2)}, u32[]{:S(2)}) collective-permute-start(bf16[512,512]{0,1:T(8,128)(2,1)S(1)} %copy.36), channel_id=1, source_target_pairs={{0,4},{4,8},{8,12},{1,5},{5,9},{9,13},{2,6},{6,10},{10,14},{3,7},{... | collective-permute-start | bytes 1572872 | tf_op jit(solution)/shard_map/ppermute | solution.py:15
  99.7 21.2 %copy-start.5 = (bf16[2560,512]{0,1:T(8,128)(2,1)}, bf16[2560,512]{0,1:T(8,128)(2,1)S(1)}, u32[]{:S(2)}) copy-start(bf16[2560,512]{0,1:T(8,128)(2,1)S(1)} %constant_dynamic-update-slice_fusion.4) | copy-start | bytes 7864324
  121.0 1.5 copy-start.3
  122.4 16.7 %copy-start.2 = (f32[4,128,128]{2,1,0:T(8,128)S(1)}, f32[4,128,128]{2,1,0:T(8,128)}, u32[]{:S(2)}) copy-start(f32[4,128,128]{2,1,0:T(8,128)} %fusion.37) | copy-start | bytes 786436
  137.7 2.1 %copy-start.1 = (bf16[512,512]{1,0:T(8,128)(2,1)S(1)}, bf16[512,512]{1,0:T(8,128)(2,1)}, u32[]{:S(2)}) copy-start(bf16[512,512]{1,0:T(8,128)(2,1)} %param.6) | copy-start | bytes 1572868
  139.8 5.2 %copy-start.4 = (bf16[2560,512]{0,1:T(8,128)(2,1)S(1)}, bf16[2560,512]{0,1:T(8,128)(2,1)}, u32[]{:S(2)}) copy-start(bf16[2560,512]{0,1:T(8,128)(2,1)} %copy-done.3) | copy-start | bytes 7864324
  145.0 17.4 %slice-start = ((s8[8388608]{0:T(1024)(128)(4,1)}), s8[4194304]{0:T(1024)(128)(4,1)S(1)}, s32[]{:S(2)}) async-start(s8[8388608]{0:T(1024)(128)(4,1)} %bitcast.96), calls=%async_computation.2 | async-start | bytes 8388608
  145.0 17.3 %slice-start.1 = ((s8[8388608]{0:T(1024)(128)(4,1)}), s8[4194304]{0:T(1024)(128)(4,1)S(1)}, s32[]{:S(2)}) async-start(s8[8388608]{0:T(1024)(128)(4,1)} %bitcast.96), calls=%async_computation.3 | async-start | bytes 8388608
Sparse Core Ops, SparseCore 0:
  20.2 60.3 all-gather.2
